TPU v7x, 32 devices: a whole 2x2x4 slice. The times are simulated.
32 devices in a mesh: wide: 16 (over z, y, core), narrow: 2 (over x).
Axes of the slice: x: 2, y: 2, z: 4, core: 2. Of those that a mesh axis runs over, the one named last changes fastest.
Arguments:
- shocks: bfloat16 [64, 4096], replicated, may hold values from -6 to 6
- load_tiles: bfloat16 [32, 128, 128], P('narrow'), may hold values from -0.5 to 0.5
- load_index: int32 [32, 2], P('narrow'), may hold values from 0 to 31, as said below
- delta_tiles: bfloat16 [1024, 128, 128], P('wide'), may hold values from -0.09375 to 0.09375
- delta_index: int32 [256, 4], P('wide'), may hold values from 0 to 31, all different within a row
- base_value: float32 [32768], P('wide'), may hold values from -3 to 3
- trade_set: int32 [32768], P('wide'), may hold values from 0 to 2047, as said below
- set_slot: int32 [2048], replicated, may hold values from 0 to 2047, as said below
- default_step: int32 [64, 2048], P('narrow', 'wide'), may hold values from 0 to 7
Outputs:
- epe: float32 [2048], P('wide')
- default_loss: float32 [2048], P('wide')
Inputs may be any that keep to these rules, and one draw needn't show every extreme that they name: load_index[i] = (row block, column block); the column blocks of the tiles of narrow index j lie in j * 16 to (j + 1) * 16 - 1, and no pair repeats. `delta_index`: the 4 factor blocks of one trade block differ. `set_slot`: A permutation of the netting sets. `trade_set`: of the 2048 trades of one index of wide, at most 256 have sets of one owner (set_slot // 128); one owner gets exactly 256 from every index of wide.
All inputs are finite; a program needn't handle non-finite values.
Results may differ from a plain program's by a relative error of at most 0.00046.
Values may be sent and summed in bfloat16 or wider, within the bound.
A program may use at most 64 MiB of HBM per device.

v0:
```python
import jax
import jax.numpy as jnp
from jax import lax
from jax.sharding import PartitionSpec as P

BLOCK = 128
STEPS = 8
STEP = 3


def on_device(
    shocks,
    load_tiles,
    load_index,
    delta_tiles,
    delta_index,
    base_value,
    trade_set,
    set_slot,
    default_step,
):
    narrow_count = lax.axis_size("narrow")
    group = lax.axis_index("narrow")
    scen_total, width = shocks.shape
    blocks_all = width // BLOCK
    own_blocks = blocks_all // narrow_count
    shock_blocks = shocks.reshape(scen_total, blocks_all, BLOCK)
    picked = jnp.take(shock_blocks, load_index[:, 0], axis=1)
    loaded = jnp.einsum("sla,lab->slb", picked, load_tiles, preferred_element_type=jnp.float32)
    target = load_index[:, 1] - group * own_blocks
    placing = (target[:, None] == jnp.arange(own_blocks, dtype=jnp.int32)[None, :]).astype(
        jnp.float32
    )
    spread = jnp.einsum("slb,lc->scb", loaded, placing, precision=lax.Precision.HIGHEST)
    own_columns = lax.dynamic_slice_in_dim(shock_blocks, group * own_blocks, own_blocks, 1).astype(
        jnp.float32
    )
    moves_own = (own_columns + spread).astype(jnp.bfloat16).reshape(scen_total, own_blocks * BLOCK)
    moves = lax.all_to_all(moves_own, "narrow", split_axis=0, concat_axis=1, tiled=True)
    scen_dev = moves.shape[0]
    move_blocks = moves.reshape(scen_dev, blocks_all, BLOCK)
    tb_count, per_block = delta_index.shape
    gathered = jnp.take(move_blocks, delta_index.reshape(-1), axis=1).reshape(
        scen_dev, tb_count, per_block, BLOCK
    )
    tile_groups = delta_tiles.reshape(tb_count, per_block, BLOCK, BLOCK)
    valued = jnp.einsum("sbka,bkat->sbt", gathered, tile_groups, preferred_element_type=jnp.float32)
    values = valued.reshape(scen_dev, tb_count * BLOCK) + base_value[None, :]
    wide_count = lax.axis_size("wide")
    own_sets = default_step.shape[1]
    slots = jnp.take(set_slot, trade_set)
    owner = slots // own_sets
    local = slots % own_sets
    capacity = 2 * trade_set.shape[0] // wide_count
    owner_hits = (owner[:, None] == jnp.arange(wide_count, dtype=jnp.int32)[None, :]).astype(
        jnp.int32
    )
    position = jnp.sum(jnp.cumsum(owner_hits, axis=0) * owner_hits, axis=1) - 1
    target_slot = owner * capacity + position
    sent_values = (
        jnp.zeros((scen_dev, wide_count * capacity), jnp.float32).at[:, target_slot].set(values)
    )
    sent_ids = (
        jnp.full((1, wide_count * capacity), float(own_sets), jnp.float32)
        .at[0, target_slot]
        .set(local.astype(jnp.float32))
    )
    got_values, got_ids = (
        lax.all_to_all(sent_values, "wide", split_axis=1, concat_axis=1, tiled=True),
        lax.all_to_all(sent_ids, "wide", split_axis=1, concat_axis=1, tiled=True),
    )
    member = (got_ids[0][None, :] == jnp.arange(own_sets, dtype=jnp.float32)[:, None]).astype(
        jnp.float32
    )
    netted = jnp.einsum("sr,nr->sn", got_values, member, precision=lax.Precision.HIGHEST)
    exposure = jnp.maximum(netted, 0.0)
    default_hit = (default_step == STEP).astype(jnp.float32)
    totals = lax.psum(
        (jnp.sum(exposure, axis=0), jnp.sum(default_hit * exposure, axis=0)), "narrow"
    )
    scen_all = scen_dev * narrow_count
    return (totals[0] / scen_all, totals[1] * (STEPS / scen_all))


def solution(mesh):
    return jax.shard_map(
        on_device,
        mesh=mesh,
        in_specs=(
            P(),
            P("narrow", None, None),
            P("narrow", None),
            P("wide", None, None),
            P("wide", None),
            P("wide"),
            P("wide"),
            P(),
            P("narrow", "wide"),
        ),
        out_specs=(P("wide"), P("wide")),
        check_vma=False,
    )
```

profile of v0, /device:TPU:0, one launch (start us, length us, event | category | flops | bytes accessed | tf_op | source)
XLA Modules:
  0.0 80.2 jit_solution(11723574881305017320)
XLA Ops:
  0.6 1.3 %copy_bitcast_fusion = bf16[64,32,128]{2,0,1:T(8,128)(2,1)S(1)} fusion(bf16[64,4096]{1,0:T(8,128)(2,1)} %param.9), kind=kLoop, calls=%fused_computation.16 | loop fusion | bytes 1048576 | tf_op jit(solution)/shard_map/reshape | solution.py:27
  2.0 0.7 and_bitcast_fusion
  2.7 0.8 subtract_bitcast_fusion
  3.4 1.1 %copy.44 = bf16[8,8,32,128]{3,2,1,0:T(8,128)(2,1)S(1)} copy(bf16[8,8,32,128]{3,1,2,0:T(8,128)(2,1)} %bitcast.73) | data formatting | bytes 1048576
  4.6 0.6 gather_fusion.1
  5.2 1.4 %convolution_bitcast_fusion.1 = f32[64,16,128]{2,0,1:T(8,128)S(1)} fusion(bf16[16,128,128]{2,1,0:T(8,128)(2,1)} %param.10, bf16[16,64,128]{2,1,0:T(8,128)(2,1)S(1)} %gather_fusion.1, pred[16]{0:T(512)(128)(4,1)S(1)} %and_bitcast_fusion), kind=kOutput, calls=%fused_computation.9 | convolution fusion | flops 33685504 | bytes 1310736 | tf_op jit(solution)/shard_map/sla,lab->slb/dot_general | solution.py:29
  6.6 0.7 fusion.2
  7.3 0.8 %all_to_all.26 = bf16[2,32,2048]{2,1,0:T(8,128)(2,1)} reshape(bf16[64,16,128]{2,1,0:T(8,128)(2,1)S(1)} %fusion.2) | data formatting | bytes 524288 | tf_op jit(solution)/shard_map/all_to_all | solution.py:39
  8.1 4.2 %all-to-all-start = ((bf16[2,32,2048]{2,1,0:T(8,128)(2,1)}), bf16[2,32,2048]{2,1,0:T(8,128)(2,1)S(1)}, u32[]{:S(2)}, u32[]{:S(2)}) async-start(bf16[2,32,2048]{2,1,0:T(8,128)(2,1)} %all_to_all.26), calls=%async_computation | async-start | bytes 524288 | tf_op jit(solution)/shard_map/all_to_all | solution.py:39
  12.5 11.8 %gather_fusion = s32[2048]{0:T(1024)S(1)} fusion(s32[2048]{0:T(1024)S(1)} %copy-done.1, s32[2048]{0:T(1024)S(1)} %fusion.26), kind=kCustom, calls=%fused_computation | custom fusion | bytes 24576 | tf_op jit(solution)/shard_map/jit(_take)/gather | solution.py:51
  24.3 4.5 %reduce-window.6 = s32[16,16,128]{2,1,0:T(8,128)S(1)} reduce-window(s32[16,16,128]{2,1,0:T(8,128)S(1)} %fusion.18, s32[]{:T(128)} %constant.84.clone.1), window={size=1x1x128 pad=0_0x0_0x127_0}, to_apply=%region_0.1 | reduce-window | flops 4161536 | bytes 262148 | tf_op jit(solution)/shard_map/reduce-window
  28.8 0.4 slice_reduce_fusion
  30.4 0.7 gather_fusion.2
  31.1 0.5 convolution_bitcast_fusion.2
  31.9 7.0 %scatter_custom_fusion = f32[32,4096]{0,1:T(8,128)} fusion(s32[2048]{0:T(1024)S(1)} %compare_select_fusion, f32[2048,32]{1,0:T(8,128)S(1)} %copy.36, f32[]{:T(128)} %constant.64.clone.1), kind=kCustom, calls=%fused_computation.14 | custom fusion | bytes 524292 | tf_op jit(solution)/shard_map/scatter | solution.py:61
  39.0 3.0 %copy.37 = f32[32,16,256]{2,0,1:T(8,128)} copy(f32[32,16,256]{0,2,1:T(8,128)} %bitcast.71) | data formatting | bytes 1048576 | tf_op jit(solution)/shard_map/all_to_all | solution.py:69
  42.0 6.6 %all-to-all-start.1 = ((f32[32,16,256]{2,0,1:T(8,128)}), f32[32,16,256]{2,0,1:T(8,128)S(1)}, u32[]{:S(2)}, u32[]{:S(2)}) async-start(f32[32,16,256]{2,0,1:T(8,128)} %copy.37), calls=%async_computation.1 | async-start | bytes 1048576 | tf_op jit(solution)/shard_map/all_to_all | solution.py:69
  48.9 8.6 %scatter_custom_fusion.1 = f32[4096]{0:T(1024)} fusion(s32[2048]{0:T(1024)S(1)} %broadcast_select_fusion, f32[2048]{0:T(1024)S(1)} %get-tuple-element.6, f32[]{:T(128)} %constant.99.clone.1), kind=kCustom, calls=%fused_computation.47 | custom fusion | bytes 16388
  57.5 5.4 %all-to-all-done.1 = f32[32,16,256]{2,0,1:T(8,128)S(1)} async-done(((f32[32,16,256]{2,0,1:T(8,128)}), f32[32,16,256]{2,0,1:T(8,128)S(1)}, u32[]{:S(2)}, u32[]{:S(2)}) %all-to-all-start.1) | async-done | bytes 524320 | tf_op jit(solution)/shard_map/all_to_all | solution.py:69
  62.9 4.2 %all-to-all-start.2 = ((f32[1,16,256]{2,0,1:T(1,128)}), f32[1,16,256]{2,0,1:T(1,128)S(1)}, u32[]{:S(2)}, u32[]{:S(2)}) async-start(f32[1,16,256]{2,0,1:T(1,128)} %bitcast.20), calls=%async_computation.2 | async-start | bytes 32768 | tf_op jit(solution)/shard_map/all_to_all | solution.py:70
  67.1 6.5 %all-to-all-done.2 = f32[1,16,256]{2,0,1:T(1,128)S(1)} async-done(((f32[1,16,256]{2,0,1:T(1,128)}), f32[1,16,256]{2,0,1:T(1,128)S(1)}, u32[]{:S(2)}, u32[]{:S(2)}) %all-to-all-start.2) | async-done | bytes 16416 | tf_op jit(solution)/shard_map/all_to_all | solution.py:70
  73.6 1.2 %select_reduce_fusion = (f32[128]{0:T(128)S(1)}, f32[128]{0:T(128)S(1)}) fusion(s32[32,128]{1,0:T(8,128)S(1)} %copy-done.7, f32[32,4096]{1,0:T(8,128)S(1)} %bitcast.77, f32[4096]{0:T(1024)S(1)} %bitcast.83), kind=kOutput, calls=%fused_computation.40 | convolution fusion | flops 201871104 | bytes 558080 | tf_op jit(solution)/shard_map/sr,nr->sn/dot_general | solution.py:75
  74.8 4.9 %all-reduce.1 = (f32[128]{0:T(128)S(1)}, f32[128]{0:T(128)S(1)}) all-reduce(f32[128]{0:T(128)S(1)} %get-tuple-element.3, f32[128]{0:T(128)S(1)} %get-tuple-element.2), channel_id=1, replica_groups=mesh['wide'=16,'narrow'=2] {'narrow'}, use_global_device_ids=true, to_apply=%region_6.7 | all-reduce | flops 256 | bytes 2048 | tf_op jit(solution)/shard_map/psum | solution.py:78
  79.7 0.5 broadcast_multiply_fusion
  (40 shorter events, 1.9 us)
Async XLA Ops:
  0.6 30.5 %copy-start = (bf16[64,128,128]{2,1,0:T(8,128)(2,1)S(1)}, bf16[64,128,128]{2,1,0:T(8,128)(2,1)}, u32[]{:S(2)}) copy-start(bf16[64,128,128]{2,1,0:T(8,128)(2,1)} %param.12) | copy-start | bytes 6291460
  4.6 7.8 %copy-start.4 = (s32[16,4]{0,1:T(4,128)S(1)}, s32[16,4]{0,1:T(4,128)}, u32[]{:S(2)}) copy-start(s32[16,4]{0,1:T(4,128)} %param.13) | copy-start | bytes 772
  4.6 7.8 %copy-start.2 = (s32[2048]{0:T(1024)S(1)}, s32[2048]{0:T(1024)}, u32[]{:S(2)}) copy-start(s32[2048]{0:T(1024)} %param.15) | copy-start | bytes 24580
  4.6 7.8 %copy-start.1 = (s32[2048]{0:T(1024)S(1)}, s32[2048]{0:T(1024)}, u32[]{:S(2)}) copy-start(s32[2048]{0:T(1024)} %param.16) | copy-start | bytes 24580
  8.1 21.7 %all-to-all-start = ((bf16[2,32,2048]{2,1,0:T(8,128)(2,1)}), bf16[2,32,2048]{2,1,0:T(8,128)(2,1)S(1)}, u32[]{:S(2)}, u32[]{:S(2)}) async-start(bf16[2,32,2048]{2,1,0:T(8,128)(2,1)} %all_to_all.26), calls=%async_computation | async-start | bytes 524288 | tf_op jit(solution)/shard_map/all_to_all | solution.py:39
  30.4 1.2 %copy-start.3 = (f32[2048]{0:T(1024)S(1)}, f32[2048]{0:T(1024)}, u32[]{:S(2)}) copy-start(f32[2048]{0:T(1024)} %param.14) | copy-start | bytes 24580
  39.0 9.7 %copy-start.5 = (s32[2]{0:T(128)S(1)}, s32[2]{0:T(128)}, u32[]{:S(2)}) copy-start(s32[2]{0:T(128)} %constant.106) | copy-start | bytes 28
  39.0 9.8 %copy-start.6 = (s32[2]{0:T(128)S(1)}, s32[2]{0:T(128)}, u32[]{:S(2)}) copy-start(s32[2]{0:T(128)} %constant.109) | copy-start | bytes 28
  39.0 34.6 %copy-start.7 = (s32[32,128]{1,0:T(8,128)S(1)}, s32[32,128]{1,0:T(8,128)}, u32[]{:S(2)}) copy-start(s32[32,128]{1,0:T(8,128)} %param.17) | copy-start | bytes 49156
  42.0 20.9 %all-to-all-start.1 = ((f32[32,16,256]{2,0,1:T(8,128)}), f32[32,16,256]{2,0,1:T(8,128)S(1)}, u32[]{:S(2)}, u32[]{:S(2)}) async-start(f32[32,16,256]{2,0,1:T(8,128)} %copy.37), calls=%async_computation.1 | async-start | bytes 1048576 | tf_op jit(solution)/shard_map/all_to_all | solution.py:69
  62.9 10.7 %all-to-all-start.2 = ((f32[1,16,256]{2,0,1:T(1,128)}), f32[1,16,256]{2,0,1:T(1,128)S(1)}, u32[]{:S(2)}, u32[]{:S(2)}) async-start(f32[1,16,256]{2,0,1:T(1,128)} %bitcast.20), calls=%async_computation.2 | async-start | bytes 32768 | tf_op jit(solution)/shard_map/all_to_all | solution.py:70
where the time goes:
time: 80.7 us; the launch traced here: 80.2 us
  local copies, waits for them, and re-layouts  36.6 us (45%)
  starting transfers between devices  15 us (19%)
  waiting for transfers between devices  11.9 us (15%)
  other arithmetic  7.14 us (9%)
  blocking collectives  4.93 us (6%)
  matrix products  3.71 us (5%)
  between operations  0.91 us (1%)
    gather x1, local copies, waits for them, and re-layouts, on_device(): slots = jnp.take(set_slot, trade_set)  11.8 us
    unnamed x19, local copies, waits for them, and re-layouts  9.88 us
    scatter x1, local copies, waits for them, and re-layouts, on_device(): jnp.zeros((scen_dev, wide_count * capacity), jnp.float32).at[:, target_slot]  7.03 us
    all_to_all x1, starting transfers between devices, on_device(): lax.all_to_all(sent_values, 'wide', split_axis=1, concat_axis=1, tiled=True)  6.63 us
    all_to_all x1, waiting for transfers between devices, on_device(): lax.all_to_all(sent_ids, 'wide', split_axis=1, concat_axis=1, tiled=True)  6.45 us
    all_to_all x1, waiting for transfers between devices, on_device(): lax.all_to_all(sent_values, 'wide', split_axis=1, concat_axis=1, tiled=True)  5.43 us
    psum x1, blocking collectives, on_device(): lax.psum((jnp.sum(exposure, axis=0), jnp.sum(default_hit * exposure, axis...  4.93 us
    another operation x3, other arithmetic  4.82 us
  transfers between devices with their start and end apart: 3, of which 2 were waited for; matrix products, arithmetic and copies ran while one was open for 33% of the time, Pallas kernels for 0%

commit v1 on v0

--- a/solution.py
+++ b/solution.py
@@ -66,7 +66,12 @@
         .set(local.astype(jnp.float32))
     )
     got_values, got_ids = (
-        lax.all_to_all(sent_values, "wide", split_axis=1, concat_axis=1, tiled=True),
+        jnp.concatenate(
+            lax.all_to_all(
+                jnp.stack(jnp.split(sent_values, lax.axis_size("wide"), axis=1)), "wide", 0, 0
+            ),
+            axis=1,
+        ),
         lax.all_to_all(sent_ids, "wide", split_axis=1, concat_axis=1, tiled=True),
     )
     member = (got_ids[0][None, :] == jnp.arange(own_sets, dtype=jnp.float32)[:, None]).astype(

time: 80.7 us -> 102 us (1.26)
  local copies, waits for them, and re-layouts: 36.6 us -> 56.3 us
    another operation x0 -> x18, local copies, waits for them, and re-layouts: none -> 13 us  [on_device(): jnp.stack(jnp.split(sent_values, lax.axis_size('wide'), axis=1))]
    unnamed x19 -> x46, local copies, waits for them, and re-layouts: 9.88 us -> 19.7 us
    all_to_all x2 -> x0, local copies, waits for them, and re-layouts: 3.04 us -> none  [on_device(): lax.all_to_all(sent_values, 'wide', split_axis=1, concat_axis=1, tiled=True)]
  transfers between devices with their start and end apart: 3 -> 3, of which waited for: 2 -> 2; matrix products, arithmetic and copies ran while one was open for 33% -> 26% of each run, Pallas kernels for 0% -> 0%
where the time goes in v1:
time: 102 us; the launch traced here: 101 us
  local copies, waits for them, and re-layouts  56.3 us (55%)
  starting transfers between devices  15 us (15%)
  waiting for transfers between devices  11.9 us (12%)
  other arithmetic  7.79 us (8%)
  blocking collectives  4.93 us (5%)
  matrix products  4.42 us (4%)
    unnamed x46, local copies, waits for them, and re-layouts  19.7 us
    another operation x18, local copies, waits for them, and re-layouts, on_device(): jnp.stack(jnp.split(sent_values, lax.axis_size('wide'), axis=1))  13 us
    gather x1, local copies, waits for them, and re-layouts, on_device(): slots = jnp.take(set_slot, trade_set)  11.8 us
    scatter x1, local copies, waits for them, and re-layouts, on_device(): jnp.zeros((scen_dev, wide_count * capacity), jnp.float32).at[:, target_slot]  7.03 us
    all_to_all x1, starting transfers between devices, on_device(): lax.all_to_all(jnp.stack(jnp.split(sent_values, lax.axis_size('wide'), ax...  6.64 us
    all_to_all x1, waiting for transfers between devices, on_device(): lax.all_to_all(sent_ids, 'wide', split_axis=1, concat_axis=1, tiled=True)  6.45 us
    all_to_all x1, waiting for transfers between devices, on_device(): lax.all_to_all(jnp.stack(jnp.split(sent_values, lax.axis_size('wide'), ax...  5.43 us
    psum x1, blocking collectives, on_device(): lax.psum((jnp.sum(exposure, axis=0), jnp.sum(default_hit * exposure, axis...  4.93 us
  transfers between devices with their start and end apart: 3, of which 2 were waited for; matrix products, arithmetic and copies ran while one was open for 26% of the time, Pallas kernels for 0%

profile of v1, /device:TPU:0, one launch (start us, length us, event | category | flops | bytes accessed | tf_op | source)
XLA Modules:
  0.0 101.3 jit_solution(5487933590164059761)
XLA Ops:
  0.6 0.8 and_bitcast_fusion
  1.5 0.8 subtract_bitcast_fusion
  2.2 0.8 copy.48
  3.1 1.2 %copy_bitcast_fusion = bf16[64,32,128]{2,0,1:T(8,128)(2,1)S(1)} fusion(bf16[64,4096]{1,0:T(8,128)(2,1)} %param.9), kind=kLoop, calls=%fused_computation.16 | loop fusion | bytes 1048576 | tf_op jit(solution)/shard_map/reshape | solution.py:27
  4.3 1.1 %copy.74 = bf16[8,8,32,128]{3,2,1,0:T(8,128)(2,1)S(1)} copy(bf16[8,8,32,128]{3,1,2,0:T(8,128)(2,1)} %bitcast.106) | data formatting | bytes 1048576
  6.1 1.4 %convolution_bitcast_fusion.1 = f32[64,16,128]{2,0,1:T(8,128)S(1)} fusion(bf16[16,128,128]{2,1,0:T(8,128)(2,1)} %param.10, bf16[16,64,128]{2,1,0:T(8,128)(2,1)S(1)} %gather_fusion.1, pred[16]{0:T(512)(128)(4,1)S(1)} %and_bitcast_fusion), kind=kOutput, calls=%fused_computation.9 | convolution fusion | flops 33685504 | bytes 1310736 | tf_op jit(solution)/shard_map/sla,lab->slb/dot_general | solution.py:29
  8.2 0.8 all_to_all.21
  9.0 4.2 %all-to-all-start = ((bf16[2,32,2048]{2,1,0:T(8,128)(2,1)}), bf16[2,32,2048]{2,1,0:T(8,128)(2,1)S(1)}, u32[]{:S(2)}, u32[]{:S(2)}) async-start(bf16[2,32,2048]{2,1,0:T(8,128)(2,1)} %all_to_all.21), calls=%async_computation | async-start | bytes 524288 | tf_op jit(solution)/shard_map/all_to_all | solution.py:39
  13.3 11.8 %gather_fusion = s32[2048]{0:T(1024)S(1)} fusion(s32[2048]{0:T(1024)S(1)} %copy-done.1, s32[2048]{0:T(1024)S(1)} %fusion.26), kind=kCustom, calls=%fused_computation | custom fusion | bytes 24576 | tf_op jit(solution)/shard_map/jit(_take)/gather | solution.py:51
  25.2 4.5 %reduce-window.6 = s32[16,16,128]{2,1,0:T(8,128)S(1)} reduce-window(s32[16,16,128]{2,1,0:T(8,128)S(1)} %fusion.18, s32[]{:T(128)} %constant.84.clone.1), window={size=1x1x128 pad=0_0x0_0x127_0}, to_apply=%region_0.1 | reduce-window | flops 4161536 | bytes 262148 | tf_op jit(solution)/shard_map/reduce-window
  32.6 7.0 %scatter_custom_fusion = f32[32,4096]{0,1:T(8,128)} fusion(s32[2048]{0:T(1024)S(1)} %compare_select_fusion, f32[2048,32]{1,0:T(8,128)S(1)} %copy.51, f32[]{:T(128)} %constant.64.clone.1), kind=kCustom, calls=%fused_computation.14 | custom fusion | bytes 524292 | tf_op jit(solution)/shard_map/scatter | solution.py:61
  39.6 2.5 %slice_bitcast_fusion = (f32[1,32,256]{1,2,0:T(8,128)}, f32[1,32,256]{1,2,0:T(8,128)}, f32[1,32,256]{1,2,0:T(8,128)}, f32[1,32,256]{1,2,0:T(8,128)}, f32[1,32,25...) fusion(f32[32,4096]{0,1:T(8,128)} %scatter_custom_fusion), kind=kLoop, calls=%fused_computation.29 | loop fusion | bytes 1048576 | tf_op jit(solution)/shard_map/stack | solution.py:71
  42.2 1.6 %copy.67 = f32[1,32,256]{2,1,0:T(8,128)} copy(f32[1,32,256]{1,2,0:T(8,128)} %get-tuple-element.6) | data formatting | bytes 65536 | tf_op jit(solution)/shard_map/stack | solution.py:71
  43.7 1.6 %copy.66 = f32[1,32,256]{2,1,0:T(8,128)} copy(f32[1,32,256]{1,2,0:T(8,128)} %get-tuple-element.7) | data formatting | bytes 65536 | tf_op jit(solution)/shard_map/stack | solution.py:71
  45.3 1.6 %copy.65 = f32[1,32,256]{2,1,0:T(8,128)} copy(f32[1,32,256]{1,2,0:T(8,128)} %get-tuple-element.8) | data formatting | bytes 65536 | tf_op jit(solution)/shard_map/stack | solution.py:71
  46.9 1.6 %copy.64 = f32[1,32,256]{2,1,0:T(8,128)} copy(f32[1,32,256]{1,2,0:T(8,128)} %get-tuple-element.9) | data formatting | bytes 65536 | tf_op jit(solution)/shard_map/stack | solution.py:71
  48.5 1.6 %copy.63 = f32[1,32,256]{2,1,0:T(8,128)} copy(f32[1,32,256]{1,2,0:T(8,128)} %get-tuple-element.10) | data formatting | bytes 65536 | tf_op jit(solution)/shard_map/stack | solution.py:71
  61.8 6.6 %all-to-all-start.1 = ((f32[16,32,256]{2,1,0:T(8,128)}), f32[16,32,256]{2,1,0:T(8,128)S(1)}, u32[]{:S(2)}, u32[]{:S(2)}) async-start(f32[16,32,256]{2,1,0:T(8,128)} %constant_dynamic-update-slice_fusion), calls=%async_computation.1 | async-start | bytes 1048576 | tf_op jit(solution)/shard_map/all_to_all | solution.py:70
  68.7 8.6 %scatter_custom_fusion.1 = f32[4096]{0:T(1024)} fusion(s32[2048]{0:T(1024)S(1)} %broadcast_select_fusion, f32[2048]{0:T(1024)S(1)} %get-tuple-element.22, f32[]{:T(128)} %constant.99.clone.1), kind=kCustom, calls=%fused_computation.79 | custom fusion | bytes 16388
  77.3 5.4 %all-to-all-done.1 = f32[16,32,256]{2,1,0:T(8,128)S(1)} async-done(((f32[16,32,256]{2,1,0:T(8,128)}), f32[16,32,256]{2,1,0:T(8,128)S(1)}, u32[]{:S(2)}, u32[]{:S(2)}) %all-to-all-start.1) | async-done | bytes 524320 | tf_op jit(solution)/shard_map/all_to_all | solution.py:70
  82.8 4.2 %all-to-all-start.2 = ((f32[1,16,256]{2,0,1:T(1,128)}), f32[1,16,256]{2,0,1:T(1,128)S(1)}, u32[]{:S(2)}, u32[]{:S(2)}) async-start(f32[1,16,256]{2,0,1:T(1,128)} %bitcast.36), calls=%async_computation.2 | async-start | bytes 32768 | tf_op jit(solution)/shard_map/all_to_all | solution.py:75
  87.0 6.5 %all-to-all-done.2 = f32[1,16,256]{2,0,1:T(1,128)S(1)} async-done(((f32[1,16,256]{2,0,1:T(1,128)}), f32[1,16,256]{2,0,1:T(1,128)S(1)}, u32[]{:S(2)}, u32[]{:S(2)}) %all-to-all-start.2) | async-done | bytes 16416 | tf_op jit(solution)/shard_map/all_to_all | solution.py:75
  93.4 1.9 %select_reduce_fusion = (f32[128]{0:T(128)S(1)}, f32[128]{0:T(128)S(1)}) fusion(s32[32,128]{1,0:T(8,128)} %param.17, f32[32,4096]{1,0:T(8,128)S(1)} %bitcast.110, f32[4096]{0:T(1024)S(1)} %bitcast.116), kind=kOutput, calls=%fused_computation.72 | convolution fusion | flops 201871104 | bytes 558080 | tf_op jit(solution)/shard_map/sr,nr->sn/dot_general | solution.py:80
  95.3 4.9 %all-reduce.1 = (f32[128]{0:T(128)S(1)}, f32[128]{0:T(128)S(1)}) all-reduce(f32[128]{0:T(128)S(1)} %get-tuple-element.3, f32[128]{0:T(128)S(1)} %get-tuple-element.2), channel_id=1, replica_groups=mesh['wide'=16,'narrow'=2] {'narrow'}, use_global_device_ids=true, to_apply=%region_6.7 | all-reduce | flops 256 | bytes 2048 | tf_op jit(solution)/shard_map/psum | solution.py:83
  (84 shorter events, 17.4 us)
Async XLA Ops:
  0.6 31.1 %copy-start = (bf16[64,128,128]{2,1,0:T(8,128)(2,1)S(1)}, bf16[64,128,128]{2,1,0:T(8,128)(2,1)}, u32[]{:S(2)}) copy-start(bf16[64,128,128]{2,1,0:T(8,128)(2,1)} %param.12) | copy-start | bytes 6291460
  5.4 7.8 %copy-start.11 = (s32[16,4]{0,1:T(4,128)S(1)}, s32[16,4]{0,1:T(4,128)}, u32[]{:S(2)}) copy-start(s32[16,4]{0,1:T(4,128)} %param.13) | copy-start | bytes 772
  5.4 7.9 %copy-start.9 = (s32[2048]{0:T(1024)S(1)}, s32[2048]{0:T(1024)}, u32[]{:S(2)}) copy-start(s32[2048]{0:T(1024)} %param.15) | copy-start | bytes 24580
  5.5 7.9 %copy-start.1 = (s32[2048]{0:T(1024)S(1)}, s32[2048]{0:T(1024)}, u32[]{:S(2)}) copy-start(s32[2048]{0:T(1024)} %param.16) | copy-start | bytes 24580
  9.0 21.5 %all-to-all-start = ((bf16[2,32,2048]{2,1,0:T(8,128)(2,1)}), bf16[2,32,2048]{2,1,0:T(8,128)(2,1)S(1)}, u32[]{:S(2)}, u32[]{:S(2)}) async-start(bf16[2,32,2048]{2,1,0:T(8,128)(2,1)} %all_to_all.21), calls=%async_computation | async-start | bytes 524288 | tf_op jit(solution)/shard_map/all_to_all | solution.py:39
  31.1 1.2 %copy-start.10 = (f32[2048]{0:T(1024)S(1)}, f32[2048]{0:T(1024)}, u32[]{:S(2)}) copy-start(f32[2048]{0:T(1024)} %param.14) | copy-start | bytes 24580
  50.7 8.7 %copy-start.5 = (f32[1,32,256]{2,1,0:T(8,128)S(1)}, f32[1,32,256]{2,1,0:T(8,128)}, u32[]{:S(2)}) copy-start(f32[1,32,256]{2,1,0:T(8,128)} %copy.64) | copy-start | bytes 98308
  50.7 9.3 %copy-start.4 = (f32[1,32,256]{2,1,0:T(8,128)S(1)}, f32[1,32,256]{2,1,0:T(8,128)}, u32[]{:S(2)}) copy-start(f32[1,32,256]{2,1,0:T(8,128)} %copy.65) | copy-start | bytes 98308
  50.7 9.9 %copy-start.3 = (f32[1,32,256]{2,1,0:T(8,128)S(1)}, f32[1,32,256]{2,1,0:T(8,128)}, u32[]{:S(2)}) copy-start(f32[1,32,256]{2,1,0:T(8,128)} %copy.66) | copy-start | bytes 98308
  50.7 10.5 %copy-start.2 = (f32[1,32,256]{2,1,0:T(8,128)S(1)}, f32[1,32,256]{2,1,0:T(8,128)}, u32[]{:S(2)}) copy-start(f32[1,32,256]{2,1,0:T(8,128)} %copy.67) | copy-start | bytes 98308
  51.4 6.1 %copy-start.8 = (f32[1,32,256]{2,1,0:T(8,128)S(1)}, f32[1,32,256]{2,1,0:T(8,128)}, u32[]{:S(2)}) copy-start(f32[1,32,256]{2,1,0:T(8,128)} %copy.61) | copy-start | bytes 98308
  51.4 6.8 %copy-start.7 = (f32[1,32,256]{2,1,0:T(8,128)S(1)}, f32[1,32,256]{2,1,0:T(8,128)}, u32[]{:S(2)}) copy-start(f32[1,32,256]{2,1,0:T(8,128)} %copy.62) | copy-start | bytes 98308
  51.4 7.4 %copy-start.6 = (f32[1,32,256]{2,1,0:T(8,128)S(1)}, f32[1,32,256]{2,1,0:T(8,128)}, u32[]{:S(2)}) copy-start(f32[1,32,256]{2,1,0:T(8,128)} %copy.63) | copy-start | bytes 98308
  51.6 16.9 %copy-start.12 = (s32[2]{0:T(128)S(1)}, s32[2]{0:T(128)}, u32[]{:S(2)}) copy-start(s32[2]{0:T(128)} %constant.106) | copy-start | bytes 28
  51.6 17.0 %copy-start.13 = (s32[2]{0:T(128)S(1)}, s32[2]{0:T(128)}, u32[]{:S(2)}) copy-start(s32[2]{0:T(128)} %constant.109) | copy-start | bytes 28
  61.8 20.9 %all-to-all-start.1 = ((f32[16,32,256]{2,1,0:T(8,128)}), f32[16,32,256]{2,1,0:T(8,128)S(1)}, u32[]{:S(2)}, u32[]{:S(2)}) async-start(f32[16,32,256]{2,1,0:T(8,128)} %constant_dynamic-update-slice_fusion), calls=%async_computation.1 | async-start | bytes 1048576 | tf_op jit(solution)/shard_map/all_to_all | solution.py:70
  82.8 10.7 %all-to-all-start.2 = ((f32[1,16,256]{2,0,1:T(1,128)}), f32[1,16,256]{2,0,1:T(1,128)S(1)}, u32[]{:S(2)}, u32[]{:S(2)}) async-start(f32[1,16,256]{2,0,1:T(1,128)} %bitcast.36), calls=%async_computation.2 | async-start | bytes 32768 | tf_op jit(solution)/shard_map/all_to_all | solution.py:75
